TPU v7x, 256 devices: a whole 4x4x8 slice. The times are simulated.
256 devices in a mesh: dp: 32 (over y_hi, z, core), head: 8 (over x, y_lo).
Axes of the slice: x: 4, y: 4 (y_hi: 2, y_lo: 2; y = y_hi * 2 + y_lo), z: 8, core: 2. Of those that a mesh axis runs over, the one named last changes fastest.
Arguments:
- queries: bfloat16 [24576, 8192], P(('dp', 'head')), may hold values from -6 to 6, as said below
- key_states: bfloat16 [24576, 1024], P(('dp', 'head')), may hold values from -6 to 6, as said below
- value_states: bfloat16 [24576, 1024], P(('dp', 'head')), may hold values from -6 to 6
- document_lengths: int32 [8], replicated, may hold values from 1 to 12288, 24576 in all
Outputs:
- attended: bfloat16 [24576, 8192], P(('dp', 'head'))
Inputs may be any that keep to these rules, and one draw needn't show every extreme that they name: `queries`: within this range. `key_states`: this range. `document_lengths`: the lengths sum to 24576 and the largest is exactly 12288.
All inputs are finite; a program needn't handle non-finite values.
Results may differ from a plain program's by a relative error of at most 0.008.
Values may be sent and summed in bfloat16 or wider, within the bound.
A program may use at most 128 MiB of HBM per device.

v0:
```python
import jax
import jax.numpy as jnp
from jax import lax
from jax.sharding import PartitionSpec as P

HQ = 64
HK = 8
DH = 128
NEGATIVE = -1e30


def document_starts(document_lengths, positions):
    document_ends = jnp.cumsum(document_lengths)
    return jnp.sum(
        jnp.where(document_ends[None, :] <= positions[:, None], document_lengths[None, :], 0),
        axis=1,
    )


def attend_block(state, query_set, key_block, value_block, key_first):
    maxima, totals, accumulated = state
    query_rows, query_positions, query_starts = query_set
    key_positions = key_first + jnp.arange(key_block.shape[0], dtype=jnp.int32)
    allowed = (key_positions[None, :] <= query_positions[:, None]) & (
        key_positions[None, :] >= query_starts[:, None]
    )
    score_scale = query_rows.shape[-1] ** (-0.5)
    scores = (
        jnp.einsum("qhgd,khd->qhgk", query_rows, key_block, preferred_element_type=jnp.float32)
        * score_scale
    )
    scores = jnp.where(allowed[:, None, None, :], scores, NEGATIVE)
    new_maxima = jnp.maximum(maxima, jnp.max(scores, axis=3))
    weights = jnp.where(allowed[:, None, None, :], jnp.exp(scores - new_maxima[..., None]), 0.0)
    factor = jnp.exp(maxima - new_maxima)
    totals = totals * factor + jnp.sum(weights, axis=3)
    accumulated = accumulated * factor[..., None] + jnp.einsum(
        "qhgk,khd->qhgd",
        weights.astype(jnp.bfloat16),
        value_block,
        preferred_element_type=jnp.float32,
    )
    return (new_maxima, totals, accumulated)


def visit(state, query_set, key_block, value_block, key_first):
    block_width = key_block.shape[0]
    latest = jnp.max(query_set[1])
    earliest = jnp.min(query_set[2])
    needed = (key_first >= 0) & (key_first <= latest) & (key_first + block_width - 1 >= earliest)
    return lax.cond(
        needed,
        lambda current: attend_block(current, query_set, key_block, value_block, key_first),
        lambda current: current,
        state,
    )


def on_device(queries, key_states, value_states, document_lengths):
    query_cols, key_cols, value_cols = (
        lax.all_to_all(queries, "head", split_axis=1, concat_axis=0, tiled=True),
        lax.all_to_all(key_states, "head", split_axis=1, concat_axis=0, tiled=True),
        lax.all_to_all(value_states, "head", split_axis=1, concat_axis=0, tiled=True),
    )
    shard_rows = query_cols.shape[0]
    local_kv = key_cols.shape[1] // DH
    group_heads = HQ // HK
    own_queries = query_cols.reshape(shard_rows, local_kv, group_heads, DH)
    key_heads = key_cols.reshape(shard_rows, local_kv, DH)
    value_heads = value_cols.reshape(shard_rows, local_kv, DH)
    dp_index = lax.axis_index("dp")
    offsets = jnp.arange(shard_rows, dtype=jnp.int32)
    own_positions = dp_index * shard_rows + offsets
    query_set = (own_queries, own_positions, document_starts(document_lengths, own_positions))
    set_rows = own_queries.shape[0]
    state = (
        jnp.full((set_rows, local_kv, group_heads), NEGATIVE, jnp.float32),
        jnp.zeros((set_rows, local_kv, group_heads), jnp.float32),
        jnp.zeros((set_rows, local_kv, group_heads, DH), jnp.float32),
    )
    key_piece = lax.all_gather(key_heads, "dp", axis=0, tiled=True)
    value_piece = lax.all_gather(value_heads, "dp", axis=0, tiled=True)
    block_width = min(shard_rows, key_piece.shape[0])

    def fold_step(number, inner_state):
        first_row = number * block_width
        key_block = lax.dynamic_slice_in_dim(key_piece, first_row, block_width, 0)
        value_block = lax.dynamic_slice_in_dim(value_piece, first_row, block_width, 0)
        return visit(inner_state, query_set, key_block, value_block, first_row)

    state = lax.fori_loop(0, key_piece.shape[0] // block_width, fold_step, state)
    own_state = tuple((member for member in state))
    maxima, totals, accumulated = own_state
    attended = (
        (accumulated / totals[..., None])
        .reshape(shard_rows, local_kv * group_heads * DH)
        .astype(jnp.bfloat16)
    )
    return lax.all_to_all(attended, "head", split_axis=0, concat_axis=1, tiled=True)


def solution(mesh):
    placed = (P(("dp", "head"), None), P(("dp", "head"), None), P(("dp", "head"), None), P())
    return jax.shard_map(
        on_device, mesh=mesh, in_specs=placed, out_specs=P(("dp", "head"), None), check_vma=False
    )
```

profile of v0, /device:TPU:144, one launch (start us, length us, event | category | flops | bytes accessed | tf_op | source)
XLA Modules:
  0.0 796.3 jit_solution(5520444923015914160)
XLA Ops:
  7.5 11.6 %all_to_all.64 = bf16[96,8,128]{2,0,1:T(8,128)(2,1)} all-to-all(bf16[96,8,128]{2,0,1:T(8,128)(2,1)S(1)} %copy_bitcast_fusion.1), channel_id=1, replica_groups=mesh['dp'=32,'head'=8] {'head'}, dimensions={1} | all-to-all | bytes 393216 | tf_op jit(solution)/shard_map/all_to_all | solution.py:63
  37.8 18.5 %all-to-all-done.1 = bf16[96,8,1024]{2,0,1:T(8,128)(2,1)S(1)} async-done(((bf16[96,8,1024]{2,0,1:T(8,128)(2,1)}), bf16[96,8,1024]{2,0,1:T(8,128)(2,1)S(1)}, u32[]{:S(2)}, u32[]{:S(2)}) %all-to-all-start.1) | async-done | bytes 1572896 | tf_op jit(solution)/shard_map/all_to_all | solution.py:61
  57.0 60.0 %all-gather.5.cloned.1.call-done = bf16[24576,1,128]{2,0,1:T(8,128)(2,1)} async-done(((bf16[768,1,128]{2,0,1:T(8,128)(2,1)}), bf16[24576,1,128]{2,0,1:T(8,128)(2,1)}) %all-gather.5.cloned.1.call-update) | async-done | bytes 6291472 | tf_op jit(solution)/shard_map/all_gather | solution.py:82
  125.6 84.5 %all-gather.3.cloned.1.call-done = bf16[24576,1,128]{2,0,1:T(8,128)(2,1)} async-done(((bf16[768,1,128]{2,0,1:T(8,128)(2,1)}), bf16[24576,1,128]{2,0,1:T(8,128)(2,1)}) %all-gather.3.cloned.1.call-update) | async-done | bytes 6291472 | tf_op jit(solution)/shard_map/all_gather | solution.py:81
  212.1 552.5 %while.22 = (s32[]{:T(128)}, f32[768,1,8]{0,2,1:T(8,128)S(1)}, f32[768,1,8]{0,2,1:T(8,128)S(1)}, f32[768,1,8,128]{0,3,2,1:T(8,128)}, s32[]{:T(128)}, /*index=5*/...) while((s32[]{:T(128)}, f32[768,1,8]{0,2,1:T(8,128)S(1)}, ...), condition=%wide.region_9.10_spmd.clone, body=%wide.region_4.9_spmd.clone.sunk | while | flops 2480623104 | bytes 143152528 | solution.py:91
  223.3 30.2 %conditional.3 = ((f32[768,1,8]{0,2,1:T(8,128)S(1)}, f32[768,1,8]{0,2,1:T(8,128)S(1)}, f32[768,1,8,128]{0,3,2,1:T(8,128)})) conditional(s32[]{:T(128)} %convert_element_type.37, (f32[768,1,8]{0,2,1:T(8,128)S(1)}, f32[768,1,8]{0,2,1:T(8,128)S(1)}, f32[768,1,8,128]{0,3,2,1:T(8,128)}) %tuple.77, (s32[]{:T(128)}, s32[]{:T(128)}, s32[768]{0:T(1024)S(1)}, ...), branch_computations={%region_5.5_spmd, %region_6.8_spmd} | conditional | flops 2480623104 | bytes 143149152 | solution.py:51
  242.5 10.9 %fusion.4 = f32[768,8]{0,1:T(8,128)S(1)} fusion(f32[768,768,8]{1,0,2:T(8,128)} %copy-done.1, f32[768,8]{0,1:T(8,128)S(1)} %bitcast.86, pred[768,768]{0,1:T(8,128)(4,1)S(1)} %compare_and_fusion), kind=kLoop, calls=%fused_computation.5 | loop fusion | flops 23586816 | bytes 19513344 | tf_op jit(solution)/shard_map/while/body/eval_jaxpr/cond/branch_1_fun/reduce_sum | solution.py:36
  254.7 30.2 %conditional.3 = ((f32[768,1,8]{0,2,1:T(8,128)S(1)}, f32[768,1,8]{0,2,1:T(8,128)S(1)}, f32[768,1,8,128]{0,3,2,1:T(8,128)})) conditional(s32[]{:T(128)} %convert_element_type.37, (f32[768,1,8]{0,2,1:T(8,128)S(1)}, f32[768,1,8]{0,2,1:T(8,128)S(1)}, f32[768,1,8,128]{0,3,2,1:T(8,128)}) %tuple.77, (s32[]{:T(128)}, s32[]{:T(128)}, s32[768]{0:T(1024)S(1)}, ...), branch_computations={%region_5.5_spmd, %region_6.8_spmd} | conditional | flops 2480623104 | bytes 143149152 | solution.py:51
  273.9 10.9 %fusion.4 = f32[768,8]{0,1:T(8,128)S(1)} fusion(f32[768,768,8]{1,0,2:T(8,128)} %copy-done.1, f32[768,8]{0,1:T(8,128)S(1)} %bitcast.86, pred[768,768]{0,1:T(8,128)(4,1)S(1)} %compare_and_fusion), kind=kLoop, calls=%fused_computation.5 | loop fusion | flops 23586816 | bytes 19513344 | tf_op jit(solution)/shard_map/while/body/eval_jaxpr/cond/branch_1_fun/reduce_sum | solution.py:36
  286.1 30.2 %conditional.3 = ((f32[768,1,8]{0,2,1:T(8,128)S(1)}, f32[768,1,8]{0,2,1:T(8,128)S(1)}, f32[768,1,8,128]{0,3,2,1:T(8,128)})) conditional(s32[]{:T(128)} %convert_element_type.37, (f32[768,1,8]{0,2,1:T(8,128)S(1)}, f32[768,1,8]{0,2,1:T(8,128)S(1)}, f32[768,1,8,128]{0,3,2,1:T(8,128)}) %tuple.77, (s32[]{:T(128)}, s32[]{:T(128)}, s32[768]{0:T(1024)S(1)}, ...), branch_computations={%region_5.5_spmd, %region_6.8_spmd} | conditional | flops 2480623104 | bytes 143149152 | solution.py:51
  305.3 10.9 %fusion.4 = f32[768,8]{0,1:T(8,128)S(1)} fusion(f32[768,768,8]{1,0,2:T(8,128)} %copy-done.1, f32[768,8]{0,1:T(8,128)S(1)} %bitcast.86, pred[768,768]{0,1:T(8,128)(4,1)S(1)} %compare_and_fusion), kind=kLoop, calls=%fused_computation.5 | loop fusion | flops 23586816 | bytes 19513344 | tf_op jit(solution)/shard_map/while/body/eval_jaxpr/cond/branch_1_fun/reduce_sum | solution.py:36
  317.5 30.2 %conditional.3 = ((f32[768,1,8]{0,2,1:T(8,128)S(1)}, f32[768,1,8]{0,2,1:T(8,128)S(1)}, f32[768,1,8,128]{0,3,2,1:T(8,128)})) conditional(s32[]{:T(128)} %convert_element_type.37, (f32[768,1,8]{0,2,1:T(8,128)S(1)}, f32[768,1,8]{0,2,1:T(8,128)S(1)}, f32[768,1,8,128]{0,3,2,1:T(8,128)}) %tuple.77, (s32[]{:T(128)}, s32[]{:T(128)}, s32[768]{0:T(1024)S(1)}, ...), branch_computations={%region_5.5_spmd, %region_6.8_spmd} | conditional | flops 2480623104 | bytes 143149152 | solution.py:51
  336.7 10.9 %fusion.4 = f32[768,8]{0,1:T(8,128)S(1)} fusion(f32[768,768,8]{1,0,2:T(8,128)} %copy-done.1, f32[768,8]{0,1:T(8,128)S(1)} %bitcast.86, pred[768,768]{0,1:T(8,128)(4,1)S(1)} %compare_and_fusion), kind=kLoop, calls=%fused_computation.5 | loop fusion | flops 23586816 | bytes 19513344 | tf_op jit(solution)/shard_map/while/body/eval_jaxpr/cond/branch_1_fun/reduce_sum | solution.py:36
  348.9 30.2 %conditional.3 = ((f32[768,1,8]{0,2,1:T(8,128)S(1)}, f32[768,1,8]{0,2,1:T(8,128)S(1)}, f32[768,1,8,128]{0,3,2,1:T(8,128)})) conditional(s32[]{:T(128)} %convert_element_type.37, (f32[768,1,8]{0,2,1:T(8,128)S(1)}, f32[768,1,8]{0,2,1:T(8,128)S(1)}, f32[768,1,8,128]{0,3,2,1:T(8,128)}) %tuple.77, (s32[]{:T(128)}, s32[]{:T(128)}, s32[768]{0:T(1024)S(1)}, ...), branch_computations={%region_5.5_spmd, %region_6.8_spmd} | conditional | flops 2480623104 | bytes 143149152 | solution.py:51
  368.1 10.9 %fusion.4 = f32[768,8]{0,1:T(8,128)S(1)} fusion(f32[768,768,8]{1,0,2:T(8,128)} %copy-done.1, f32[768,8]{0,1:T(8,128)S(1)} %bitcast.86, pred[768,768]{0,1:T(8,128)(4,1)S(1)} %compare_and_fusion), kind=kLoop, calls=%fused_computation.5 | loop fusion | flops 23586816 | bytes 19513344 | tf_op jit(solution)/shard_map/while/body/eval_jaxpr/cond/branch_1_fun/reduce_sum | solution.py:36
  380.3 30.2 %conditional.3 = ((f32[768,1,8]{0,2,1:T(8,128)S(1)}, f32[768,1,8]{0,2,1:T(8,128)S(1)}, f32[768,1,8,128]{0,3,2,1:T(8,128)})) conditional(s32[]{:T(128)} %convert_element_type.37, (f32[768,1,8]{0,2,1:T(8,128)S(1)}, f32[768,1,8]{0,2,1:T(8,128)S(1)}, f32[768,1,8,128]{0,3,2,1:T(8,128)}) %tuple.77, (s32[]{:T(128)}, s32[]{:T(128)}, s32[768]{0:T(1024)S(1)}, ...), branch_computations={%region_5.5_spmd, %region_6.8_spmd} | conditional | flops 2480623104 | bytes 143149152 | solution.py:51
  399.5 10.9 %fusion.4 = f32[768,8]{0,1:T(8,128)S(1)} fusion(f32[768,768,8]{1,0,2:T(8,128)} %copy-done.1, f32[768,8]{0,1:T(8,128)S(1)} %bitcast.86, pred[768,768]{0,1:T(8,128)(4,1)S(1)} %compare_and_fusion), kind=kLoop, calls=%fused_computation.5 | loop fusion | flops 23586816 | bytes 19513344 | tf_op jit(solution)/shard_map/while/body/eval_jaxpr/cond/branch_1_fun/reduce_sum | solution.py:36
  411.7 30.2 %conditional.3 = ((f32[768,1,8]{0,2,1:T(8,128)S(1)}, f32[768,1,8]{0,2,1:T(8,128)S(1)}, f32[768,1,8,128]{0,3,2,1:T(8,128)})) conditional(s32[]{:T(128)} %convert_element_type.37, (f32[768,1,8]{0,2,1:T(8,128)S(1)}, f32[768,1,8]{0,2,1:T(8,128)S(1)}, f32[768,1,8,128]{0,3,2,1:T(8,128)}) %tuple.77, (s32[]{:T(128)}, s32[]{:T(128)}, s32[768]{0:T(1024)S(1)}, ...), branch_computations={%region_5.5_spmd, %region_6.8_spmd} | conditional | flops 2480623104 | bytes 143149152 | solution.py:51
  430.9 10.9 %fusion.4 = f32[768,8]{0,1:T(8,128)S(1)} fusion(f32[768,768,8]{1,0,2:T(8,128)} %copy-done.1, f32[768,8]{0,1:T(8,128)S(1)} %bitcast.86, pred[768,768]{0,1:T(8,128)(4,1)S(1)} %compare_and_fusion), kind=kLoop, calls=%fused_computation.5 | loop fusion | flops 23586816 | bytes 19513344 | tf_op jit(solution)/shard_map/while/body/eval_jaxpr/cond/branch_1_fun/reduce_sum | solution.py:36
  443.1 30.2 %conditional.3 = ((f32[768,1,8]{0,2,1:T(8,128)S(1)}, f32[768,1,8]{0,2,1:T(8,128)S(1)}, f32[768,1,8,128]{0,3,2,1:T(8,128)})) conditional(s32[]{:T(128)} %convert_element_type.37, (f32[768,1,8]{0,2,1:T(8,128)S(1)}, f32[768,1,8]{0,2,1:T(8,128)S(1)}, f32[768,1,8,128]{0,3,2,1:T(8,128)}) %tuple.77, (s32[]{:T(128)}, s32[]{:T(128)}, s32[768]{0:T(1024)S(1)}, ...), branch_computations={%region_5.5_spmd, %region_6.8_spmd} | conditional | flops 2480623104 | bytes 143149152 | solution.py:51
  462.3 10.9 %fusion.4 = f32[768,8]{0,1:T(8,128)S(1)} fusion(f32[768,768,8]{1,0,2:T(8,128)} %copy-done.1, f32[768,8]{0,1:T(8,128)S(1)} %bitcast.86, pred[768,768]{0,1:T(8,128)(4,1)S(1)} %compare_and_fusion), kind=kLoop, calls=%fused_computation.5 | loop fusion | flops 23586816 | bytes 19513344 | tf_op jit(solution)/shard_map/while/body/eval_jaxpr/cond/branch_1_fun/reduce_sum | solution.py:36
  474.5 30.2 %conditional.3 = ((f32[768,1,8]{0,2,1:T(8,128)S(1)}, f32[768,1,8]{0,2,1:T(8,128)S(1)}, f32[768,1,8,128]{0,3,2,1:T(8,128)})) conditional(s32[]{:T(128)} %convert_element_type.37, (f32[768,1,8]{0,2,1:T(8,128)S(1)}, f32[768,1,8]{0,2,1:T(8,128)S(1)}, f32[768,1,8,128]{0,3,2,1:T(8,128)}) %tuple.77, (s32[]{:T(128)}, s32[]{:T(128)}, s32[768]{0:T(1024)S(1)}, ...), branch_computations={%region_5.5_spmd, %region_6.8_spmd} | conditional | flops 2480623104 | bytes 143149152 | solution.py:51
  493.7 10.9 %fusion.4 = f32[768,8]{0,1:T(8,128)S(1)} fusion(f32[768,768,8]{1,0,2:T(8,128)} %copy-done.1, f32[768,8]{0,1:T(8,128)S(1)} %bitcast.86, pred[768,768]{0,1:T(8,128)(4,1)S(1)} %compare_and_fusion), kind=kLoop, calls=%fused_computation.5 | loop fusion | flops 23586816 | bytes 19513344 | tf_op jit(solution)/shard_map/while/body/eval_jaxpr/cond/branch_1_fun/reduce_sum | solution.py:36
  505.9 30.2 %conditional.3 = ((f32[768,1,8]{0,2,1:T(8,128)S(1)}, f32[768,1,8]{0,2,1:T(8,128)S(1)}, f32[768,1,8,128]{0,3,2,1:T(8,128)})) conditional(s32[]{:T(128)} %convert_element_type.37, (f32[768,1,8]{0,2,1:T(8,128)S(1)}, f32[768,1,8]{0,2,1:T(8,128)S(1)}, f32[768,1,8,128]{0,3,2,1:T(8,128)}) %tuple.77, (s32[]{:T(128)}, s32[]{:T(128)}, s32[768]{0:T(1024)S(1)}, ...), branch_computations={%region_5.5_spmd, %region_6.8_spmd} | conditional | flops 2480623104 | bytes 143149152 | solution.py:51
  537.2 30.2 %conditional.3 = ((f32[768,1,8]{0,2,1:T(8,128)S(1)}, f32[768,1,8]{0,2,1:T(8,128)S(1)}, f32[768,1,8,128]{0,3,2,1:T(8,128)})) conditional(s32[]{:T(128)} %convert_element_type.37, (f32[768,1,8]{0,2,1:T(8,128)S(1)}, f32[768,1,8]{0,2,1:T(8,128)S(1)}, f32[768,1,8,128]{0,3,2,1:T(8,128)}) %tuple.77, (s32[]{:T(128)}, s32[]{:T(128)}, s32[768]{0:T(1024)S(1)}, ...), branch_computations={%region_5.5_spmd, %region_6.8_spmd} | conditional | flops 2480623104 | bytes 143149152 | solution.py:51
  568.6 30.2 %conditional.3 = ((f32[768,1,8]{0,2,1:T(8,128)S(1)}, f32[768,1,8]{0,2,1:T(8,128)S(1)}, f32[768,1,8,128]{0,3,2,1:T(8,128)})) conditional(s32[]{:T(128)} %convert_element_type.37, (f32[768,1,8]{0,2,1:T(8,128)S(1)}, f32[768,1,8]{0,2,1:T(8,128)S(1)}, f32[768,1,8,128]{0,3,2,1:T(8,128)}) %tuple.77, (s32[]{:T(128)}, s32[]{:T(128)}, s32[768]{0:T(1024)S(1)}, ...), branch_computations={%region_5.5_spmd, %region_6.8_spmd} | conditional | flops 2480623104 | bytes 143149152 | solution.py:51
  600.0 30.2 %conditional.3 = ((f32[768,1,8]{0,2,1:T(8,128)S(1)}, f32[768,1,8]{0,2,1:T(8,128)S(1)}, f32[768,1,8,128]{0,3,2,1:T(8,128)})) conditional(s32[]{:T(128)} %convert_element_type.37, (f32[768,1,8]{0,2,1:T(8,128)S(1)}, f32[768,1,8]{0,2,1:T(8,128)S(1)}, f32[768,1,8,128]{0,3,2,1:T(8,128)}) %tuple.77, (s32[]{:T(128)}, s32[]{:T(128)}, s32[768]{0:T(1024)S(1)}, ...), branch_computations={%region_5.5_spmd, %region_6.8_spmd} | conditional | flops 2480623104 | bytes 143149152 | solution.py:51
  631.4 30.2 %conditional.3 = ((f32[768,1,8]{0,2,1:T(8,128)S(1)}, f32[768,1,8]{0,2,1:T(8,128)S(1)}, f32[768,1,8,128]{0,3,2,1:T(8,128)})) conditional(s32[]{:T(128)} %convert_element_type.37, (f32[768,1,8]{0,2,1:T(8,128)S(1)}, f32[768,1,8]{0,2,1:T(8,128)S(1)}, f32[768,1,8,128]{0,3,2,1:T(8,128)}) %tuple.77, (s32[]{:T(128)}, s32[]{:T(128)}, s32[768]{0:T(1024)S(1)}, ...), branch_computations={%region_5.5_spmd, %region_6.8_spmd} | conditional | flops 2480623104 | bytes 143149152 | solution.py:51
  662.8 30.2 %conditional.3 = ((f32[768,1,8]{0,2,1:T(8,128)S(1)}, f32[768,1,8]{0,2,1:T(8,128)S(1)}, f32[768,1,8,128]{0,3,2,1:T(8,128)})) conditional(s32[]{:T(128)} %convert_element_type.37, (f32[768,1,8]{0,2,1:T(8,128)S(1)}, f32[768,1,8]{0,2,1:T(8,128)S(1)}, f32[768,1,8,128]{0,3,2,1:T(8,128)}) %tuple.77, (s32[]{:T(128)}, s32[]{:T(128)}, s32[768]{0:T(1024)S(1)}, ...), branch_computations={%region_5.5_spmd, %region_6.8_spmd} | conditional | flops 2480623104 | bytes 143149152 | solution.py:51
  694.2 30.2 %conditional.3 = ((f32[768,1,8]{0,2,1:T(8,128)S(1)}, f32[768,1,8]{0,2,1:T(8,128)S(1)}, f32[768,1,8,128]{0,3,2,1:T(8,128)})) conditional(s32[]{:T(128)} %convert_element_type.37, (f32[768,1,8]{0,2,1:T(8,128)S(1)}, f32[768,1,8]{0,2,1:T(8,128)S(1)}, f32[768,1,8,128]{0,3,2,1:T(8,128)}) %tuple.77, (s32[]{:T(128)}, s32[]{:T(128)}, s32[768]{0:T(1024)S(1)}, ...), branch_computations={%region_5.5_spmd, %region_6.8_spmd} | conditional | flops 2480623104 | bytes 143149152 | solution.py:51
  725.6 30.2 %conditional.3 = ((f32[768,1,8]{0,2,1:T(8,128)S(1)}, f32[768,1,8]{0,2,1:T(8,128)S(1)}, f32[768,1,8,128]{0,3,2,1:T(8,128)})) conditional(s32[]{:T(128)} %convert_element_type.37, (f32[768,1,8]{0,2,1:T(8,128)S(1)}, f32[768,1,8]{0,2,1:T(8,128)S(1)}, f32[768,1,8,128]{0,3,2,1:T(8,128)}) %tuple.77, (s32[]{:T(128)}, s32[]{:T(128)}, s32[768]{0:T(1024)S(1)}, ...), branch_computations={%region_5.5_spmd, %region_6.8_spmd} | conditional | flops 2480623104 | bytes 143149152 | solution.py:51
  768.6 19.6 %all_to_all.66 = bf16[8,96,1024]{2,1,0:T(8,128)(2,1)S(1)} all-to-all(bf16[8,96,1024]{2,1,0:T(8,128)(2,1)S(1)} %convert_element_type.27), channel_id=1, replica_groups=mesh['dp'=32,'head'=8] {'head'}, dimensions={0} | all-to-all | bytes 3145728 | tf_op jit(solution)/shard_map/all_to_all | solution.py:99
  (236 shorter events, 449.4 us)
Async XLA Ops:
  6.5 0.9 copy-start
  6.5 30.4 %copy-start.2 = (s32[8]{0:T(128)S(1)}, s32[8]{0:T(128)}, u32[]{:S(2)}) copy-start(s32[8]{0:T(128)} %param.11) | copy-start | bytes 100
  6.5 110.4 %all-gather.5.cloned.1.call-start = ((), (), s32[]{:S(2)}) async-start(), calls=%async_computation.5 | async-start | bytes 6488064 | tf_op jit(solution)/shard_map/all_gather | solution.py:82
  19.1 191.0 %all-gather.3.cloned.1.call-start = ((), (), s32[]{:S(2)}) async-start(), calls=%async_computation.4 | async-start | bytes 6488064 | tf_op jit(solution)/shard_map/all_gather | solution.py:81
  32.7 23.7 %all-to-all-start.1 = ((bf16[96,8,1024]{2,0,1:T(8,128)(2,1)}), bf16[96,8,1024]{2,0,1:T(8,128)(2,1)S(1)}, u32[]{:S(2)}, u32[]{:S(2)}) async-start(bf16[96,8,1024]{2,0,1:T(8,128)(2,1)} %bitcast.84), calls=%async_computation.1 | async-start | bytes 3145728 | tf_op jit(solution)/shard_map/all_to_all | solution.py:61
  228.0 6.5 copy-start.1
  259.4 6.5 copy-start.1
  290.8 6.5 copy-start.1
  322.2 6.5 copy-start.1
  353.6 6.5 copy-start.1
  384.9 6.5 copy-start.1
  416.3 6.5 copy-start.1
  447.7 6.5 copy-start.1
  479.1 6.5 copy-start.1
  510.5 6.5 copy-start.1
  541.9 6.5 copy-start.1
  573.3 6.5 copy-start.1
  604.7 6.5 copy-start.1
  636.1 6.5 copy-start.1
  667.5 6.5 copy-start.1
  698.9 6.5 copy-start.1
  730.3 6.5 copy-start.1
Sparse Core Ops, SparseCore 0:
  19.2 97.6 all-gather.4
  119.7 90.3 all-gather.2
where the time goes:
time: 799 us; the launch traced here: 796 us
  matrix products  207 us (26%)
  other arithmetic  199 us (25%)
  waiting for transfers between devices  163 us (20%)
  local copies, waits for them, and re-layouts  129 us (16%)
  loops' own time  41.2 us (5%)
  blocking collectives  40.9 us (5%)
  between operations  13.5 us (2%)
    reduce_sum x17, other arithmetic, attend_block(): totals = totals * factor + jnp.sum(weights, axis=3)  186 us
    dot_general x17, matrix products, attend_block(): jnp.einsum('qhgk,khd->qhgd', weights.astype(jnp.bfloat16), value_block, p...  137 us
    cond x51, local copies, waits for them, and re-layouts  110 us
    all_gather x1, waiting for transfers between devices, on_device(): key_piece = lax.all_gather(key_heads, 'dp', axis=0, tiled=True)  84.5 us
    dot_general x17, matrix products, attend_block(): jnp.einsum('qhgd,khd->qhgk', query_rows, key_block, preferred_element_typ...  69.6 us
    all_gather x1, waiting for transfers between devices, on_device(): value_piece = lax.all_gather(value_heads, 'dp', axis=0, tiled=True)  60 us
    another operation x1, loops' own time, on_device(): lax.fori_loop(0, key_piece.shape[0] // block_width, fold_step, state)  39.5 us
    all_to_all x1, blocking collectives, on_device(): lax.all_to_all(attended, 'head', split_axis=0, concat_axis=1, tiled=True)  19.6 us
  transfers between devices with their start and end apart: 3, of which 3 were waited for; matrix products, arithmetic and copies ran while one was open for 2% of the time, Pallas kernels for 0%

commit v1 on v0

--- a/solution.py
+++ b/solution.py
@@ -78,8 +78,11 @@
         jnp.zeros((set_rows, local_kv, group_heads), jnp.float32),
         jnp.zeros((set_rows, local_kv, group_heads, DH), jnp.float32),
     )
-    key_piece = lax.all_gather(key_heads, "dp", axis=0, tiled=True)
-    value_piece = lax.all_gather(value_heads, "dp", axis=0, tiled=True)
+    key_piece, value_piece = jnp.split(
+        lax.all_gather(jnp.concatenate([key_heads, value_heads], axis=1), "dp", axis=0, tiled=True),
+        [key_heads.shape[1]],
+        axis=1,
+    )
     block_width = min(shard_rows, key_piece.shape[0])
 
     def fold_step(number, inner_state):

time: 799 us -> 761 us (0.952)
  waiting for transfers between devices: 163 us -> 118 us
  local copies, waits for them, and re-layouts: 129 us -> 142 us
  blocking collectives: 40.9 us -> 29.2 us
    all_gather x2 -> x1, waiting for transfers between devices: 144 us -> 93.6 us  [on_device(): lax.all_gather(jnp.concatenate([key_heads, value_heads], axis=1), 'dp', a...]
    split x0 -> x1, local copies, waits for them, and re-layouts: none -> 10.1 us  [on_device(): jnp.split(lax.all_gather(jnp.concatenate([key_heads, value_heads], axis=1...]
    all_to_all x1 -> x0, blocking collectives: 9.75 us -> none  [on_device(): lax.all_to_all(key_states, 'head', split_axis=1, concat_axis=0, tiled=True)]
  transfers between devices with their start and end apart: 3 -> 3, of which waited for: 3 -> 3; matrix products, arithmetic and copies ran while one was open for 2% -> 1% of each run, Pallas kernels for 0% -> 0%
where the time goes in v1:
time: 761 us; the launch traced here: 758 us
  matrix products  207 us (27%)
  other arithmetic  201 us (26%)
  local copies, waits for them, and re-layouts  142 us (19%)
  waiting for transfers between devices  118 us (16%)
  loops' own time  40.1 us (5%)
  blocking collectives  29.2 us (4%)
  between operations  13.5 us (2%)
  starting transfers between devices  8.64 us (1%)
    reduce_sum x17, other arithmetic, attend_block(): totals = totals * factor + jnp.sum(weights, axis=3)  186 us
    dot_general x17, matrix products, attend_block(): jnp.einsum('qhgk,khd->qhgd', weights.astype(jnp.bfloat16), value_block, p...  137 us
    cond x51, local copies, waits for them, and re-layouts  109 us
    all_gather x1, waiting for transfers between devices, on_device(): lax.all_gather(jnp.concatenate([key_heads, value_heads], axis=1), 'dp', a...  93.6 us
    dot_general x17, matrix products, attend_block(): jnp.einsum('qhgd,khd->qhgk', query_rows, key_block, preferred_element_typ...  70.1 us
    another operation x1, loops' own time, on_device(): lax.fori_loop(0, key_piece.shape[0] // block_width, fold_step, state)  38.5 us
    all_to_all x1, blocking collectives, on_device(): lax.all_to_all(attended, 'head', split_axis=0, concat_axis=1, tiled=True)  19.7 us
    all_to_all x1, waiting for transfers between devices, on_device(): lax.all_to_all(queries, 'head', split_axis=1, concat_axis=0, tiled=True)  18.3 us
  transfers between devices with their start and end apart: 3, of which 3 were waited for; matrix products, arithmetic and copies ran while one was open for 1% of the time, Pallas kernels for 0%

profile of v1, /device:TPU:144, one launch (start us, length us, event | category | flops | bytes accessed | tf_op | source)
XLA Modules:
  0.0 758.5 jit_solution(10067797988877403500)
XLA Ops:
  38.0 18.3 %all-to-all-done.2 = bf16[96,8,1024]{2,0,1:T(8,128)(2,1)S(1)} async-done(((bf16[96,8,1024]{2,0,1:T(8,128)(2,1)}), bf16[96,8,1024]{2,0,1:T(8,128)(2,1)S(1)}, u32[]{:S(2)}, u32[]{:S(2)}) %all-to-all-start.2) | async-done | bytes 1572896 | tf_op jit(solution)/shard_map/all_to_all | solution.py:61
  56.9 93.6 %all-gather.2.cloned.1.call-done = bf16[24576,2,128]{2,0,1:T(8,128)(2,1)} async-done(((bf16[768,2,128]{2,0,1:T(8,128)(2,1)}), bf16[24576,2,128]{2,0,1:T(8,128)(2,1)}) %all-gather.2.cloned.1.call-update) | async-done | bytes 12582928 | tf_op jit(solution)/shard_map/all_gather | solution.py:82
  171.2 551.9 %while.22 = (s32[]{:T(128)}, f32[768,1,8]{0,2,1:T(8,128)S(1)}, f32[768,1,8]{0,2,1:T(8,128)S(1)}, f32[768,1,8,128]{0,3,2,1:T(8,128)}, s32[]{:T(128)}, /*index=5*/...) while((s32[]{:T(128)}, f32[768,1,8]{0,2,1:T(8,128)S(1)}, ...), condition=%wide.region_9.10_spmd.clone, body=%wide.region_4.9_spmd.clone.sunk | while | flops 2480623104 | bytes 143152528 | solution.py:94
  182.2 30.2 %conditional.3 = ((f32[768,1,8]{0,2,1:T(8,128)S(1)}, f32[768,1,8]{0,2,1:T(8,128)S(1)}, f32[768,1,8,128]{0,3,2,1:T(8,128)})) conditional(s32[]{:T(128)} %convert_element_type.37, (f32[768,1,8]{0,2,1:T(8,128)S(1)}, f32[768,1,8]{0,2,1:T(8,128)S(1)}, f32[768,1,8,128]{0,3,2,1:T(8,128)}) %tuple.80, (s32[]{:T(128)}, s32[]{:T(128)}, s32[768]{0:T(1024)S(1)}, ...), branch_computations={%region_5.5_spmd, %region_6.8_spmd} | conditional | flops 2480623104 | bytes 143149152 | solution.py:51
  201.4 10.9 %fusion.4 = f32[768,8]{0,1:T(8,128)S(1)} fusion(f32[768,768,8]{1,0,2:T(8,128)} %copy-done.2, f32[768,8]{0,1:T(8,128)S(1)} %bitcast.86, pred[768,768]{0,1:T(8,128)(4,1)S(1)} %compare_and_fusion), kind=kLoop, calls=%fused_computation.5 | loop fusion | flops 23586816 | bytes 19513344 | tf_op jit(solution)/shard_map/while/body/eval_jaxpr/cond/branch_1_fun/reduce_sum | solution.py:36
  213.5 30.2 %conditional.3 = ((f32[768,1,8]{0,2,1:T(8,128)S(1)}, f32[768,1,8]{0,2,1:T(8,128)S(1)}, f32[768,1,8,128]{0,3,2,1:T(8,128)})) conditional(s32[]{:T(128)} %convert_element_type.37, (f32[768,1,8]{0,2,1:T(8,128)S(1)}, f32[768,1,8]{0,2,1:T(8,128)S(1)}, f32[768,1,8,128]{0,3,2,1:T(8,128)}) %tuple.80, (s32[]{:T(128)}, s32[]{:T(128)}, s32[768]{0:T(1024)S(1)}, ...), branch_computations={%region_5.5_spmd, %region_6.8_spmd} | conditional | flops 2480623104 | bytes 143149152 | solution.py:51
  232.7 10.9 %fusion.4 = f32[768,8]{0,1:T(8,128)S(1)} fusion(f32[768,768,8]{1,0,2:T(8,128)} %copy-done.2, f32[768,8]{0,1:T(8,128)S(1)} %bitcast.86, pred[768,768]{0,1:T(8,128)(4,1)S(1)} %compare_and_fusion), kind=kLoop, calls=%fused_computation.5 | loop fusion | flops 23586816 | bytes 19513344 | tf_op jit(solution)/shard_map/while/body/eval_jaxpr/cond/branch_1_fun/reduce_sum | solution.py:36
  244.9 30.2 %conditional.3 = ((f32[768,1,8]{0,2,1:T(8,128)S(1)}, f32[768,1,8]{0,2,1:T(8,128)S(1)}, f32[768,1,8,128]{0,3,2,1:T(8,128)})) conditional(s32[]{:T(128)} %convert_element_type.37, (f32[768,1,8]{0,2,1:T(8,128)S(1)}, f32[768,1,8]{0,2,1:T(8,128)S(1)}, f32[768,1,8,128]{0,3,2,1:T(8,128)}) %tuple.80, (s32[]{:T(128)}, s32[]{:T(128)}, s32[768]{0:T(1024)S(1)}, ...), branch_computations={%region_5.5_spmd, %region_6.8_spmd} | conditional | flops 2480623104 | bytes 143149152 | solution.py:51
  264.1 10.9 %fusion.4 = f32[768,8]{0,1:T(8,128)S(1)} fusion(f32[768,768,8]{1,0,2:T(8,128)} %copy-done.2, f32[768,8]{0,1:T(8,128)S(1)} %bitcast.86, pred[768,768]{0,1:T(8,128)(4,1)S(1)} %compare_and_fusion), kind=kLoop, calls=%fused_computation.5 | loop fusion | flops 23586816 | bytes 19513344 | tf_op jit(solution)/shard_map/while/body/eval_jaxpr/cond/branch_1_fun/reduce_sum | solution.py:36
  276.3 30.2 %conditional.3 = ((f32[768,1,8]{0,2,1:T(8,128)S(1)}, f32[768,1,8]{0,2,1:T(8,128)S(1)}, f32[768,1,8,128]{0,3,2,1:T(8,128)})) conditional(s32[]{:T(128)} %convert_element_type.37, (f32[768,1,8]{0,2,1:T(8,128)S(1)}, f32[768,1,8]{0,2,1:T(8,128)S(1)}, f32[768,1,8,128]{0,3,2,1:T(8,128)}) %tuple.80, (s32[]{:T(128)}, s32[]{:T(128)}, s32[768]{0:T(1024)S(1)}, ...), branch_computations={%region_5.5_spmd, %region_6.8_spmd} | conditional | flops 2480623104 | bytes 143149152 | solution.py:51
  295.5 10.9 %fusion.4 = f32[768,8]{0,1:T(8,128)S(1)} fusion(f32[768,768,8]{1,0,2:T(8,128)} %copy-done.2, f32[768,8]{0,1:T(8,128)S(1)} %bitcast.86, pred[768,768]{0,1:T(8,128)(4,1)S(1)} %compare_and_fusion), kind=kLoop, calls=%fused_computation.5 | loop fusion | flops 23586816 | bytes 19513344 | tf_op jit(solution)/shard_map/while/body/eval_jaxpr/cond/branch_1_fun/reduce_sum | solution.py:36
  307.7 30.2 %conditional.3 = ((f32[768,1,8]{0,2,1:T(8,128)S(1)}, f32[768,1,8]{0,2,1:T(8,128)S(1)}, f32[768,1,8,128]{0,3,2,1:T(8,128)})) conditional(s32[]{:T(128)} %convert_element_type.37, (f32[768,1,8]{0,2,1:T(8,128)S(1)}, f32[768,1,8]{0,2,1:T(8,128)S(1)}, f32[768,1,8,128]{0,3,2,1:T(8,128)}) %tuple.80, (s32[]{:T(128)}, s32[]{:T(128)}, s32[768]{0:T(1024)S(1)}, ...), branch_computations={%region_5.5_spmd, %region_6.8_spmd} | conditional | flops 2480623104 | bytes 143149152 | solution.py:51
  326.9 10.9 %fusion.4 = f32[768,8]{0,1:T(8,128)S(1)} fusion(f32[768,768,8]{1,0,2:T(8,128)} %copy-done.2, f32[768,8]{0,1:T(8,128)S(1)} %bitcast.86, pred[768,768]{0,1:T(8,128)(4,1)S(1)} %compare_and_fusion), kind=kLoop, calls=%fused_computation.5 | loop fusion | flops 23586816 | bytes 19513344 | tf_op jit(solution)/shard_map/while/body/eval_jaxpr/cond/branch_1_fun/reduce_sum | solution.py:36
  339.1 30.2 %conditional.3 = ((f32[768,1,8]{0,2,1:T(8,128)S(1)}, f32[768,1,8]{0,2,1:T(8,128)S(1)}, f32[768,1,8,128]{0,3,2,1:T(8,128)})) conditional(s32[]{:T(128)} %convert_element_type.37, (f32[768,1,8]{0,2,1:T(8,128)S(1)}, f32[768,1,8]{0,2,1:T(8,128)S(1)}, f32[768,1,8,128]{0,3,2,1:T(8,128)}) %tuple.80, (s32[]{:T(128)}, s32[]{:T(128)}, s32[768]{0:T(1024)S(1)}, ...), branch_computations={%region_5.5_spmd, %region_6.8_spmd} | conditional | flops 2480623104 | bytes 143149152 | solution.py:51
  358.3 10.9 %fusion.4 = f32[768,8]{0,1:T(8,128)S(1)} fusion(f32[768,768,8]{1,0,2:T(8,128)} %copy-done.2, f32[768,8]{0,1:T(8,128)S(1)} %bitcast.86, pred[768,768]{0,1:T(8,128)(4,1)S(1)} %compare_and_fusion), kind=kLoop, calls=%fused_computation.5 | loop fusion | flops 23586816 | bytes 19513344 | tf_op jit(solution)/shard_map/while/body/eval_jaxpr/cond/branch_1_fun/reduce_sum | solution.py:36
  370.5 30.2 %conditional.3 = ((f32[768,1,8]{0,2,1:T(8,128)S(1)}, f32[768,1,8]{0,2,1:T(8,128)S(1)}, f32[768,1,8,128]{0,3,2,1:T(8,128)})) conditional(s32[]{:T(128)} %convert_element_type.37, (f32[768,1,8]{0,2,1:T(8,128)S(1)}, f32[768,1,8]{0,2,1:T(8,128)S(1)}, f32[768,1,8,128]{0,3,2,1:T(8,128)}) %tuple.80, (s32[]{:T(128)}, s32[]{:T(128)}, s32[768]{0:T(1024)S(1)}, ...), branch_computations={%region_5.5_spmd, %region_6.8_spmd} | conditional | flops 2480623104 | bytes 143149152 | solution.py:51
  389.7 10.9 %fusion.4 = f32[768,8]{0,1:T(8,128)S(1)} fusion(f32[768,768,8]{1,0,2:T(8,128)} %copy-done.2, f32[768,8]{0,1:T(8,128)S(1)} %bitcast.86, pred[768,768]{0,1:T(8,128)(4,1)S(1)} %compare_and_fusion), kind=kLoop, calls=%fused_computation.5 | loop fusion | flops 23586816 | bytes 19513344 | tf_op jit(solution)/shard_map/while/body/eval_jaxpr/cond/branch_1_fun/reduce_sum | solution.py:36
  401.8 30.2 %conditional.3 = ((f32[768,1,8]{0,2,1:T(8,128)S(1)}, f32[768,1,8]{0,2,1:T(8,128)S(1)}, f32[768,1,8,128]{0,3,2,1:T(8,128)})) conditional(s32[]{:T(128)} %convert_element_type.37, (f32[768,1,8]{0,2,1:T(8,128)S(1)}, f32[768,1,8]{0,2,1:T(8,128)S(1)}, f32[768,1,8,128]{0,3,2,1:T(8,128)}) %tuple.80, (s32[]{:T(128)}, s32[]{:T(128)}, s32[768]{0:T(1024)S(1)}, ...), branch_computations={%region_5.5_spmd, %region_6.8_spmd} | conditional | flops 2480623104 | bytes 143149152 | solution.py:51
  421.1 10.9 %fusion.4 = f32[768,8]{0,1:T(8,128)S(1)} fusion(f32[768,768,8]{1,0,2:T(8,128)} %copy-done.2, f32[768,8]{0,1:T(8,128)S(1)} %bitcast.86, pred[768,768]{0,1:T(8,128)(4,1)S(1)} %compare_and_fusion), kind=kLoop, calls=%fused_computation.5 | loop fusion | flops 23586816 | bytes 19513344 | tf_op jit(solution)/shard_map/while/body/eval_jaxpr/cond/branch_1_fun/reduce_sum | solution.py:36
  433.2 30.2 %conditional.3 = ((f32[768,1,8]{0,2,1:T(8,128)S(1)}, f32[768,1,8]{0,2,1:T(8,128)S(1)}, f32[768,1,8,128]{0,3,2,1:T(8,128)})) conditional(s32[]{:T(128)} %convert_element_type.37, (f32[768,1,8]{0,2,1:T(8,128)S(1)}, f32[768,1,8]{0,2,1:T(8,128)S(1)}, f32[768,1,8,128]{0,3,2,1:T(8,128)}) %tuple.80, (s32[]{:T(128)}, s32[]{:T(128)}, s32[768]{0:T(1024)S(1)}, ...), branch_computations={%region_5.5_spmd, %region_6.8_spmd} | conditional | flops 2480623104 | bytes 143149152 | solution.py:51
  452.4 10.9 %fusion.4 = f32[768,8]{0,1:T(8,128)S(1)} fusion(f32[768,768,8]{1,0,2:T(8,128)} %copy-done.2, f32[768,8]{0,1:T(8,128)S(1)} %bitcast.86, pred[768,768]{0,1:T(8,128)(4,1)S(1)} %compare_and_fusion), kind=kLoop, calls=%fused_computation.5 | loop fusion | flops 23586816 | bytes 19513344 | tf_op jit(solution)/shard_map/while/body/eval_jaxpr/cond/branch_1_fun/reduce_sum | solution.py:36
  464.6 30.2 %conditional.3 = ((f32[768,1,8]{0,2,1:T(8,128)S(1)}, f32[768,1,8]{0,2,1:T(8,128)S(1)}, f32[768,1,8,128]{0,3,2,1:T(8,128)})) conditional(s32[]{:T(128)} %convert_element_type.37, (f32[768,1,8]{0,2,1:T(8,128)S(1)}, f32[768,1,8]{0,2,1:T(8,128)S(1)}, f32[768,1,8,128]{0,3,2,1:T(8,128)}) %tuple.80, (s32[]{:T(128)}, s32[]{:T(128)}, s32[768]{0:T(1024)S(1)}, ...), branch_computations={%region_5.5_spmd, %region_6.8_spmd} | conditional | flops 2480623104 | bytes 143149152 | solution.py:51
  483.8 10.9 %fusion.4 = f32[768,8]{0,1:T(8,128)S(1)} fusion(f32[768,768,8]{1,0,2:T(8,128)} %copy-done.2, f32[768,8]{0,1:T(8,128)S(1)} %bitcast.86, pred[768,768]{0,1:T(8,128)(4,1)S(1)} %compare_and_fusion), kind=kLoop, calls=%fused_computation.5 | loop fusion | flops 23586816 | bytes 19513344 | tf_op jit(solution)/shard_map/while/body/eval_jaxpr/cond/branch_1_fun/reduce_sum | solution.py:36
  496.0 30.2 %conditional.3 = ((f32[768,1,8]{0,2,1:T(8,128)S(1)}, f32[768,1,8]{0,2,1:T(8,128)S(1)}, f32[768,1,8,128]{0,3,2,1:T(8,128)})) conditional(s32[]{:T(128)} %convert_element_type.37, (f32[768,1,8]{0,2,1:T(8,128)S(1)}, f32[768,1,8]{0,2,1:T(8,128)S(1)}, f32[768,1,8,128]{0,3,2,1:T(8,128)}) %tuple.80, (s32[]{:T(128)}, s32[]{:T(128)}, s32[768]{0:T(1024)S(1)}, ...), branch_computations={%region_5.5_spmd, %region_6.8_spmd} | conditional | flops 2480623104 | bytes 143149152 | solution.py:51
  527.4 30.2 %conditional.3 = ((f32[768,1,8]{0,2,1:T(8,128)S(1)}, f32[768,1,8]{0,2,1:T(8,128)S(1)}, f32[768,1,8,128]{0,3,2,1:T(8,128)})) conditional(s32[]{:T(128)} %convert_element_type.37, (f32[768,1,8]{0,2,1:T(8,128)S(1)}, f32[768,1,8]{0,2,1:T(8,128)S(1)}, f32[768,1,8,128]{0,3,2,1:T(8,128)}) %tuple.80, (s32[]{:T(128)}, s32[]{:T(128)}, s32[768]{0:T(1024)S(1)}, ...), branch_computations={%region_5.5_spmd, %region_6.8_spmd} | conditional | flops 2480623104 | bytes 143149152 | solution.py:51
  558.8 30.2 %conditional.3 = ((f32[768,1,8]{0,2,1:T(8,128)S(1)}, f32[768,1,8]{0,2,1:T(8,128)S(1)}, f32[768,1,8,128]{0,3,2,1:T(8,128)})) conditional(s32[]{:T(128)} %convert_element_type.37, (f32[768,1,8]{0,2,1:T(8,128)S(1)}, f32[768,1,8]{0,2,1:T(8,128)S(1)}, f32[768,1,8,128]{0,3,2,1:T(8,128)}) %tuple.80, (s32[]{:T(128)}, s32[]{:T(128)}, s32[768]{0:T(1024)S(1)}, ...), branch_computations={%region_5.5_spmd, %region_6.8_spmd} | conditional | flops 2480623104 | bytes 143149152 | solution.py:51
  590.1 30.2 %conditional.3 = ((f32[768,1,8]{0,2,1:T(8,128)S(1)}, f32[768,1,8]{0,2,1:T(8,128)S(1)}, f32[768,1,8,128]{0,3,2,1:T(8,128)})) conditional(s32[]{:T(128)} %convert_element_type.37, (f32[768,1,8]{0,2,1:T(8,128)S(1)}, f32[768,1,8]{0,2,1:T(8,128)S(1)}, f32[768,1,8,128]{0,3,2,1:T(8,128)}) %tuple.80, (s32[]{:T(128)}, s32[]{:T(128)}, s32[768]{0:T(1024)S(1)}, ...), branch_computations={%region_5.5_spmd, %region_6.8_spmd} | conditional | flops 2480623104 | bytes 143149152 | solution.py:51
  621.5 30.2 %conditional.3 = ((f32[768,1,8]{0,2,1:T(8,128)S(1)}, f32[768,1,8]{0,2,1:T(8,128)S(1)}, f32[768,1,8,128]{0,3,2,1:T(8,128)})) conditional(s32[]{:T(128)} %convert_element_type.37, (f32[768,1,8]{0,2,1:T(8,128)S(1)}, f32[768,1,8]{0,2,1:T(8,128)S(1)}, f32[768,1,8,128]{0,3,2,1:T(8,128)}) %tuple.80, (s32[]{:T(128)}, s32[]{:T(128)}, s32[768]{0:T(1024)S(1)}, ...), branch_computations={%region_5.5_spmd, %region_6.8_spmd} | conditional | flops 2480623104 | bytes 143149152 | solution.py:51
  640.8 10.9 %fusion.4 = f32[768,8]{0,1:T(8,128)S(1)} fusion(f32[768,768,8]{1,0,2:T(8,128)} %copy-done.2, f32[768,8]{0,1:T(8,128)S(1)} %bitcast.86, pred[768,768]{0,1:T(8,128)(4,1)S(1)} %compare_and_fusion), kind=kLoop, calls=%fused_computation.5 | loop fusion | flops 23586816 | bytes 19513344 | tf_op jit(solution)/shard_map/while/body/eval_jaxpr/cond/branch_1_fun/reduce_sum | solution.py:36
  652.9 30.2 %conditional.3 = ((f32[768,1,8]{0,2,1:T(8,128)S(1)}, f32[768,1,8]{0,2,1:T(8,128)S(1)}, f32[768,1,8,128]{0,3,2,1:T(8,128)})) conditional(s32[]{:T(128)} %convert_element_type.37, (f32[768,1,8]{0,2,1:T(8,128)S(1)}, f32[768,1,8]{0,2,1:T(8,128)S(1)}, f32[768,1,8,128]{0,3,2,1:T(8,128)}) %tuple.80, (s32[]{:T(128)}, s32[]{:T(128)}, s32[768]{0:T(1024)S(1)}, ...), branch_computations={%region_5.5_spmd, %region_6.8_spmd} | conditional | flops 2480623104 | bytes 143149152 | solution.py:51
  684.3 30.2 %conditional.3 = ((f32[768,1,8]{0,2,1:T(8,128)S(1)}, f32[768,1,8]{0,2,1:T(8,128)S(1)}, f32[768,1,8,128]{0,3,2,1:T(8,128)})) conditional(s32[]{:T(128)} %convert_element_type.37, (f32[768,1,8]{0,2,1:T(8,128)S(1)}, f32[768,1,8]{0,2,1:T(8,128)S(1)}, f32[768,1,8,128]{0,3,2,1:T(8,128)}) %tuple.80, (s32[]{:T(128)}, s32[]{:T(128)}, s32[768]{0:T(1024)S(1)}, ...), branch_computations={%region_5.5_spmd, %region_6.8_spmd} | conditional | flops 2480623104 | bytes 143149152 | solution.py:51
  730.6 19.7 %all_to_all.65 = bf16[8,96,1024]{2,1,0:T(8,128)(2,1)S(1)} all-to-all(bf16[8,96,1024]{2,1,0:T(8,128)(2,1)} %convert_element_type.27), channel_id=1, replica_groups=mesh['dp'=32,'head'=8] {'head'}, dimensions={0} | all-to-all | bytes 3145728 | tf_op jit(solution)/shard_map/all_to_all | solution.py:102
  (237 shorter events, 453.3 us)
Async XLA Ops:
  6.5 0.9 copy-start
  7.5 29.0 %copy-start.3 = (s32[8]{0:T(128)S(1)}, s32[8]{0:T(128)}, u32[]{:S(2)}) copy-start(s32[8]{0:T(128)} %param.11) | copy-start | bytes 100
  8.2 11.7 %all-to-all-start = ((bf16[96,8,128]{2,0,1:T(8,128)(2,1)}), bf16[96,8,128]{2,0,1:T(8,128)(2,1)S(1)}, u32[]{:S(2)}, u32[]{:S(2)}) async-start(bf16[96,8,128]{2,0,1:T(8,128)(2,1)} %copy_bitcast_fusion.2), calls=%async_computation | async-start | bytes 393216 | tf_op jit(solution)/shard_map/all_to_all | solution.py:62
  13.2 137.3 %all-gather.2.cloned.1.call-start = ((), (), s32[]{:S(2)}) async-start(), calls=%async_computation.4 | async-start | bytes 12976128 | tf_op jit(solution)/shard_map/all_gather | solution.py:82
  32.9 23.4 %all-to-all-start.2 = ((bf16[96,8,1024]{2,0,1:T(8,128)(2,1)}), bf16[96,8,1024]{2,0,1:T(8,128)(2,1)S(1)}, u32[]{:S(2)}, u32[]{:S(2)}) async-start(bf16[96,8,1024]{2,0,1:T(8,128)(2,1)} %bitcast.84), calls=%async_computation.2 | async-start | bytes 3145728 | tf_op jit(solution)/shard_map/all_to_all | solution.py:61
  186.8 6.5 copy-start.2
  218.2 6.5 copy-start.2
  249.6 6.5 copy-start.2
  281.0 6.5 copy-start.2
  312.4 6.5 copy-start.2
  343.8 6.5 copy-start.2
  375.2 6.5 copy-start.2
  406.5 6.5 copy-start.2
  437.9 6.5 copy-start.2
  469.3 6.5 copy-start.2
  500.7 6.5 copy-start.2
  532.1 6.5 copy-start.2
  563.5 6.5 copy-start.2
  594.9 6.5 copy-start.2
  626.2 6.5 copy-start.2
  657.6 6.5 copy-start.2
  689.0 6.5 copy-start.2
  723.1 28.6 %copy-start.1 = (bf16[96,1024]{1,0:T(8,128)(2,1)S(1)}, bf16[96,1024]{1,0:T(8,128)(2,1)}, u32[]{:S(2)}) copy-start(bf16[96,1024]{1,0:T(8,128)(2,1)} %param.9) | copy-start | bytes 589828
Sparse Core Ops, SparseCore 0:
  30.3 120.2 all-gather.1
